TPU v7x, 32 devices: a whole 2x2x4 slice. The times are simulated.
32 devices in a mesh: dom: 8 (over z, y), cluster: 4 (over x, core).
Axes of the slice: x: 2, y: 2, z: 4, core: 2. Of those that a mesh axis runs over, the one named last changes fastest.
Arguments:
- features: bfloat16 [4, 6144, 512], P('cluster', 'dom'), may hold values from -6 to 6
- stale: bfloat16 [4, 256, 512], P('cluster'), may hold values from -6 to 6
- boundary: int32 [4, 8], P('cluster', 'dom'), may hold values from 0 to 23
- skip: int32 [4, 8], P('cluster'), may hold values 0 or 1
- tile_vals: bfloat16 [4, 256, 32, 128], P('cluster', 'dom'), may hold values from -0.4375 to 0.4375
- tile_row: int32 [4, 256], P('cluster', 'dom'), may hold values from 0 to 5
- tile_src: int32 [4, 256], P('cluster', 'dom'), may hold values from 0 to 9
- tile_count: int32 [4, 8], P('cluster', 'dom'), may hold values from 16 to 32, as said below
- weight: bfloat16 [512, 512], replicated, may hold values from -0.25 to 0.25
- cotangent: bfloat16 [4, 6144, 512], P('cluster', 'dom'), may hold values from -6 to 6
Outputs:
- out_features: bfloat16 [4, 6144, 512], P('cluster', 'dom')
- grad_features: bfloat16 [4, 6144, 512], P('cluster', 'dom')
- grad_weight: float32 [512, 512], P('dom')
Inputs may be any that keep to these rules, and one draw needn't show every extreme that they name: `tile_count`: every partition has at least half of its slots live; some partition has all 32 slots live.
All inputs are finite; a program needn't handle non-finite values. No bound on the sum of `skip` on one device may be relied on, other than what follows from the above.
Results may differ from a plain program's by a relative error of at most 0.02.
Values may be sent and summed in bfloat16 or wider, within the bound.
A program may use at most 64 MiB of HBM per device.

v0:
```python
import jax
import jax.numpy as jnp
from jax import lax
from jax.sharding import PartitionSpec as P


def padded(cells, sides, width):
    for axis, dim in sides:
        count = lax.axis_size(axis)
        head = lax.slice_in_dim(cells, 0, width, axis=dim)
        tail = lax.slice_in_dim(cells, cells.shape[dim] - width, cells.shape[dim], axis=dim)
        cells = jnp.concatenate(
            [
                lax.ppermute(tail, axis, [(i, (i + 1) % count) for i in range(count)]),
                cells,
                lax.ppermute(head, axis, [((i + 1) % count, i) for i in range(count)]),
            ],
            axis=dim,
        )
    return cells


def passed_along(x, axis, by):
    count = lax.axis_size(axis)
    return lax.ppermute(x, axis, [(i, (i + by) % count) for i in range(count)])


def silu_parts(value):
    sig = jax.nn.sigmoid(value)
    return (value * sig, sig * (1.0 + value * (1.0 - sig)))


def per_device(
    features, stale, boundary, skip, tile_vals, tile_row, tile_src, tile_count, weight, cotangent
):
    feats = features[0]
    nodes, width = feats.shape
    parts = lax.axis_size("dom")
    blk = stale.shape[1] // parts
    tile_blocks = tile_vals[0]
    slots, _, tile_rows = tile_blocks.shape
    row_blocks = nodes // tile_rows
    start_row = boundary[0, 0] * blk
    own_block = lax.dynamic_slice_in_dim(feats, start_row, blk, 0)
    gathered = lax.all_gather(own_block, "dom", axis=0, tiled=True).reshape(parts, blk, width)
    beside_all = padded(own_block[None], (("cluster", 0),), 1)
    skipped = skip[0] == 1
    fresh = jnp.where(skipped[:, None, None], stale[0].reshape(parts, blk, width), gathered)
    table = jnp.concatenate([fresh, beside_all[0:1], beside_all[2:3]], axis=0)
    active_mask = (jnp.arange(slots, dtype=jnp.int32) < tile_count[0, 0]).astype(jnp.float32)
    sources = tile_src[0]
    targets = tile_row[0]
    selected_block = jnp.take(table, sources, axis=0)
    contribution = (
        jnp.einsum("wnz,wnx->wzx", tile_blocks, selected_block, preferred_element_type=jnp.float32)
        * active_mask[:, None, None]
    )
    row_onehot_mask = (targets[:, None] == jnp.arange(row_blocks, dtype=jnp.int32)[None, :]).astype(
        jnp.float32
    )
    row_onehot_mask = row_onehot_mask * active_mask[:, None]
    aggregate_block_list = jnp.einsum(
        "xn,xij->nij", row_onehot_mask, contribution, precision=lax.Precision.HIGHEST
    )
    agg = (feats.astype(jnp.float32) + aggregate_block_list.reshape(nodes, width)).astype(
        jnp.bfloat16
    )
    zval = jnp.dot(agg, weight, preferred_element_type=jnp.float32)
    act, slope = silu_parts(zval)
    out_features = act.astype(jnp.bfloat16)
    dz = (cotangent[0].astype(jnp.float32) * slope).astype(jnp.bfloat16)
    dagg = lax.dot_general(
        dz, weight, (((1,), (1,)), ((), ())), preferred_element_type=jnp.float32
    ).astype(jnp.bfloat16)
    selected_rows = jnp.take(dagg.reshape(row_blocks, tile_rows, width), targets, axis=0)
    selected_gradient = (
        jnp.einsum("dck,dkn->dcn", tile_blocks, selected_rows, preferred_element_type=jnp.float32)
        * active_mask[:, None, None]
    )
    src_hot = (sources[:, None] == jnp.arange(parts + 2, dtype=jnp.int32)[None, :]).astype(
        jnp.float32
    )
    dsrc = jnp.einsum("ts,tbf->sbf", src_hot, selected_gradient, precision=lax.Precision.HIGHEST)
    keep = 1.0 - skipped.astype(jnp.float32)
    in_group = dsrc[:parts] * keep[:, None, None]
    from_upper = passed_along(dsrc[parts].astype(jnp.bfloat16), "cluster", -1).astype(jnp.float32)
    from_lower = passed_along(dsrc[parts + 1].astype(jnp.bfloat16), "cluster", 1).astype(
        jnp.float32
    )
    share = width // parts
    term_all = lax.dot_general(
        agg, dz, (((0,), (0,)), ((), ())), preferred_element_type=jnp.float32
    ).reshape(parts, share, width)
    stacked = jnp.concatenate([in_group, term_all], axis=1).reshape(parts * (blk + share), width)
    summed = lax.psum_scatter(
        stacked.astype(jnp.bfloat16), "dom", scatter_dimension=0, tiled=True
    ).astype(jnp.float32)
    mine = summed[:blk]
    grad_weight = lax.psum(summed[blk:].astype(jnp.bfloat16), "cluster").astype(jnp.float32)
    bgrad = mine + from_upper + from_lower
    full = dagg.astype(jnp.float32)
    current = lax.dynamic_slice_in_dim(full, start_row, blk, 0)
    full = lax.dynamic_update_slice_in_dim(full, current + bgrad, start_row, 0)
    grad_features = full.astype(jnp.bfloat16)
    return (out_features[None], grad_features[None], grad_weight)


def solution(mesh):
    return jax.shard_map(
        per_device,
        mesh=mesh,
        in_specs=(
            P("cluster", "dom", None),
            P("cluster", None, None),
            P("cluster", "dom"),
            P("cluster", None),
            P("cluster", "dom", None, None),
            P("cluster", "dom"),
            P("cluster", "dom"),
            P("cluster", "dom"),
            P(),
            P("cluster", "dom", None),
        ),
        out_specs=(P("cluster", "dom", None), P("cluster", "dom", None), P("dom", None)),
        check_vma=False,
    )
```

profile of v0, /device:TPU:0, one launch (start us, length us, event | category | flops | bytes accessed | tf_op | source)
XLA Modules:
  0.0 193.5 jit_solution(16718258283287903912)
XLA Ops:
  7.2 0.0 copy-start
  7.2 0.0 reduce-scatter.2.cloned.1.call-start
  8.0 0.8 constant_dynamic-slice_fusion
  8.7 0.5 collective-permute-start
  9.2 1.9 collective-permute-start.1
  11.1 31.9 %all-gather = bf16[1,256,512]{2,1,0:T(8,128)(2,1)S(1)} all-gather(bf16[1,32,512]{2,1,0:T(8,128)(2,1)S(1)} %constant_dynamic-slice_fusion), channel_id=2, replica_groups=mesh['dom'=8,'cluster'=4] {'dom'}, dimensions={1}, use_global_device_ids=true | all-gather | bytes 294912 | tf_op jit(solution)/shard_map/all_gather | solution.py:45
  43.0 0.7 fusion.30
  43.7 0.7 compare_and_fusion.1
  44.3 0.7 fusion.31
  45.0 0.7 compare_and_fusion
  45.7 0.7 compare_bitcast_fusion
  46.3 0.7 convert_subtract_fusion
  47.7 1.1 broadcast_select_fusion
  48.7 0.0 collective-permute-done
  48.7 0.0 collective-permute-done.1
  48.8 0.6 gather_fusion
  49.4 4.6 %fusion.13 = f32[32,512,128]{2,1,0:T(8,128)} fusion(bf16[32,32,512]{2,1,0:T(8,128)(2,1)S(1)} %gather_fusion, pred[32]{0:T(512)(128)(4,1)S(1)} %compare_and_fusion.1, bf16[1,32,32,128]{3,2,1,0:T(8,128)(2,1)S(1)} %copy-done.1), kind=kOutput, calls=%fused_computation.22 | convolution fusion | flops 134742016 | bytes 9699360 | tf_op jit(solution)/shard_map/wnz,wnx->wzx/dot_general | solution.py:55
  54.1 10.3 %copy.20 = f32[32,512,128]{1,0,2:T(8,128)} copy(f32[32,512,128]{2,1,0:T(8,128)} %fusion.13) | data formatting | bytes 16777216 | tf_op jit(solution)/shard_map/wnz,wnx->wzx/dot_general | solution.py:55
  64.4 6.8 %fusion = f32[6,128,512]{2,0,1:T(8,128)S(1)} fusion(f32[32,512,128]{1,0,2:T(8,128)} %copy.20, f32[32]{0:T(128)S(1)} %compare_convert_fusion, s32[32]{0:T(128)S(1)} %bitcast.72), kind=kOutput, calls=%fused_computation.2 | convolution fusion | flops 153092480 | bytes 9961728 | tf_op jit(solution)/shard_map/xn,xij->nij/dot_general | solution.py:62
  71.2 0.0 copy-start.2
  71.2 0.9 copy.16
  72.1 0.2 copy-done.2
  72.3 0.3 fusion.11
  72.6 1.2 copy.17
  73.8 2.0 %fusion.10 = (bf16[768,512]{1,0:T(8,128)(2,1)S(1)}, bf16[1,768,512]{2,1,0:T(8,128)(2,1)}) fusion(bf16[1,768,512]{2,1,0:T(8,128)(2,1)S(1)} %copy-done.7, bf16[768,512]{1,0:T(8,128)(2,1)S(1)} %fusion.11, bf16[512,512]{1,0:T(8,128)(2,1)S(1)} %copy-done), kind=kOutput, calls=%fused_computation.14 | convolution fusion | flops 407371776 | bytes 3670016 | tf_op jit(solution)/shard_map/dot_general | solution.py:68
  75.8 0.6 fusion.35
  76.4 0.5 copy-done.3
  76.9 1.4 convolution_convert_fusion.1
  78.3 2.8 %gather_fusion.1 = bf16[32,128,512]{2,1,0:T(8,128)(2,1)} fusion(bf16[6,128,512]{2,1,0:T(8,128)(2,1)S(1)} %bitcast.66, s32[1024]{0:T(1024)S(1)} %pad_clamp_fusion), kind=kCustom, calls=%fused_computation.1 | custom fusion | bytes 8388736 | tf_op jit(solution)/shard_map/jit(_take)/gather | solution.py:75
  81.0 3.1 %fusion.3 = f32[32,512,32]{1,2,0:T(8,128)S(1)} fusion(bf16[32,128,512]{2,1,0:T(8,128)(2,1)} %gather_fusion.1, pred[32]{0:T(512)(128)(4,1)S(1)} %compare_and_fusion, bf16[1,32,32,128]{3,2,1,0:T(8,128)(2,1)S(1)} %copy-done.1), kind=kOutput, calls=%fused_computation.5 | convolution fusion | flops 136314880 | bytes 6553632 | tf_op jit(solution)/shard_map/dck,dkn->dcn/dot_general | solution.py:77
  84.2 0.0 copy-start.4
  84.2 2.0 %fusion.7 = f32[10,32,512]{2,0,1:T(8,128)S(1)} fusion(f32[32,512,32]{1,2,0:T(8,128)S(1)} %fusion.3, f32[32]{0:T(128)S(1)} %compare_convert_fusion, s32[32]{0:T(128)S(1)} %bitcast.73), kind=kOutput, calls=%fused_computation.9 | convolution fusion | flops 63439168 | bytes 2752768 | tf_op jit(solution)/shard_map/ts,tbf->sbf/dot_general | solution.py:83
  86.2 0.1 fusion.18
  86.3 0.1 copy.18
  86.4 1.0 pad_maximum_fusion
  87.4 0.0 reduce-scatter.2.cloned.1.call-update
  87.4 0.0 all-reduce.2.cloned.1.call-start
  87.4 0.4 copy.27
  87.8 0.1 collective-permute-start.2
  87.9 0.5 collective-permute-start.3
  88.4 63.3 %reduce-scatter.2.cloned.1.call-done = bf16[96,512]{1,0:T(8,128)(2,1)} async-done(((bf16[768,512]{1,0:T(8,128)(2,1)}), bf16[96,512]{1,0:T(8,128)(2,1)}) %reduce-scatter.2.cloned.1.call-update) | async-done | bytes 98320 | tf_op jit(solution)/shard_map/reduce_scatter | solution.py:95
  151.7 1.5 slice.35
  153.2 0.0 all-reduce.2.cloned.1.call-update
  153.2 0.0 collective-permute-done.2
  153.2 0.8 add_dynamic-update-slice_fusion
  154.0 1.0 convert_bitcast_fusion
  155.0 30.2 %all-reduce.2.cloned.1.call-done = bf16[64,512]{1,0:T(8,128)(2,1)} async-done(((bf16[64,512]{1,0:T(8,128)(2,1)}), bf16[64,512]{1,0:T(8,128)(2,1)}) %all-reduce.2.cloned.1.call-update) | async-done | bytes 65552 | tf_op jit(solution)/shard_map/psum | solution.py:99
  185.2 1.5 convert_element_type.90
  (17 shorter events, 0.1 us)
Async XLA Ops:
  7.2 66.6 %copy-start = (bf16[512,512]{1,0:T(8,128)(2,1)S(1)}, bf16[512,512]{1,0:T(8,128)(2,1)}, u32[]{:S(2)}) copy-start(bf16[512,512]{1,0:T(8,128)(2,1)} %param.18) | copy-start | bytes 1572868
  7.2 42.2 %copy-start.1 = (bf16[1,32,32,128]{3,2,1,0:T(8,128)(2,1)S(1)}, bf16[1,32,32,128]{3,2,1,0:T(8,128)(2,1)}, u32[]{:S(2)}) copy-start(bf16[1,32,32,128]{3,2,1,0:T(8,128)(2,1)} %param.14) | copy-start | bytes 786436
  7.2 144.5 %reduce-scatter.2.cloned.1.call-start = ((), (), s32[]{:S(2)}) async-start(), calls=%async_computation.1 | async-start | bytes 884736 | tf_op jit(solution)/shard_map/reduce_scatter | solution.py:95
  8.7 40.0 %collective-permute-start = (bf16[1,32,512]{2,1,0:T(8,128)(2,1)S(1)}, bf16[1,32,512]{2,1,0:T(8,128)(2,1)S(1)}, u32[]{:S(2)}, u32[]{:S(2)}) collective-permute-start(bf16[1,32,512]{2,1,0:T(8,128)(2,1)S(1)} %constant_dynamic-slice_fusion), channel_id=1, source_target_pairs={{0,1},{1,2},{2,3},{3,0},{4,5},{5,6},{6,7},{7,4},{8,9},{9,10},{10,1... | collective-permute-start | bytes 98312 | tf_op jit(solution)/shard_map/ppermute | solution.py:14
  9.2 39.5 %collective-permute-start.1 = (bf16[1,32,512]{2,1,0:T(8,128)(2,1)S(1)}, bf16[1,32,512]{2,1,0:T(8,128)(2,1)S(1)}, u32[]{:S(2)}, u32[]{:S(2)}) collective-permute-start(bf16[1,32,512]{2,1,0:T(8,128)(2,1)S(1)} %constant_dynamic-slice_fusion), channel_id=1, source_target_pairs={{1,0},{2,1},{3,2},{0,3},{5,4},{6,5},{7,6},{4,7},{9,8},{10,9},{11,1... | collective-permute-start | bytes 98312 | tf_op jit(solution)/shard_map/ppermute | solution.py:16
  54.0 10.3 %copy-start.5 = (s32[1,32]{1,0:T(1,128)S(1)}, s32[1,32]{1,0:T(1,128)}, u32[]{:S(2)}) copy-start(s32[1,32]{1,0:T(1,128)} %param.15) | copy-start | bytes 388
  71.2 1.1 copy-start.2
  72.3 1.5 copy-start.7
  75.8 1.1 copy-start.3
  81.0 3.1 %copy-start.6 = (s32[1,32]{1,0:T(1,128)S(1)}, s32[1,32]{1,0:T(1,128)}, u32[]{:S(2)}) copy-start(s32[1,32]{1,0:T(1,128)} %param.16) | copy-start | bytes 388
  84.2 2.2 %copy-start.4 = (bf16[8,64,512]{2,1,0:T(8,128)(2,1)S(1)}, bf16[8,64,512]{2,1,0:T(8,128)(2,1)}, u32[]{:S(2)}) copy-start(bf16[8,64,512]{2,1,0:T(8,128)(2,1)} %convolution_convert_fusion.1) | copy-start | bytes 1572868
  87.4 97.8 %all-reduce.2.cloned.1.call-start = ((), (), s32[]{:S(2)}) async-start(), calls=%async_computation.2 | async-start | bytes 131072 | tf_op jit(solution)/shard_map/psum | solution.py:99
  87.8 65.4 %collective-permute-start.2 = (bf16[32,512]{1,0:T(8,128)(2,1)S(1)}, bf16[32,512]{1,0:T(8,128)(2,1)S(1)}, u32[]{:S(2)}, u32[]{:S(2)}) collective-permute-start(bf16[32,512]{1,0:T(8,128)(2,1)S(1)} %get-tuple-element.5), channel_id=1, source_target_pairs={{0,3},{1,0},{2,1},{3,2},{4,7},{5,4},{6,5},{7,6},{8,11},{9,8},{10,9... | collective-permute-start | bytes 98312 | tf_op jit(solution)/shard_map/ppermute | solution.py:25
  87.9 65.3 %collective-permute-start.3 = (bf16[32,512]{1,0:T(8,128)(2,1)S(1)}, bf16[32,512]{1,0:T(8,128)(2,1)S(1)}, u32[]{:S(2)}, u32[]{:S(2)}) collective-permute-start(bf16[32,512]{1,0:T(8,128)(2,1)S(1)} %get-tuple-element.6), channel_id=1, source_target_pairs={{0,1},{1,2},{2,3},{3,0},{4,5},{5,6},{6,7},{7,4},{8,9},{9,10},{10,1... | collective-permute-start | bytes 98312 | tf_op jit(solution)/shard_map/ppermute | solution.py:25
Sparse Core Ops, SparseCore 0:
  87.5 64.1 reduce-scatter.1
  154.6 30.5 all-reduce.1
where the time goes:
time: 194 us
  waiting for transfers between devices  93.6 us (48%)
  blocking collectives  31.9 us (16%)
  matrix products  20.5 us (11%)
  local copies, waits for them, and re-layouts  19.2 us (10%)
  between operations  15.6 us (8%)
  other arithmetic  9.72 us (5%)
  starting transfers between devices  3.04 us (2%)
    reduce_scatter x1, waiting for transfers between devices, per_device(): lax.psum_scatter(stacked.astype(jnp.bfloat16), 'dom', scatter_dimension=0...  63.3 us
    all_gather x1, blocking collectives, per_device(): lax.all_gather(own_block, 'dom', axis=0, tiled=True)  31.9 us
    psum x1, waiting for transfers between devices, per_device(): lax.psum(summed[blk:].astype(jnp.bfloat16), 'cluster').astype(jnp.float32)  30.2 us
    dot_general x1, local copies, waits for them, and re-layouts, per_device(): jnp.einsum('wnz,wnx->wzx', tile_blocks, selected_block, preferred_element...  10.3 us
    dot_general x1, matrix products, per_device(): jnp.einsum('xn,xij->nij', row_onehot_mask, contribution, precision=lax.Pr...  6.78 us
    dot_general x1, matrix products, per_device(): jnp.einsum('wnz,wnx->wzx', tile_blocks, selected_block, preferred_element...  4.61 us
  transfers between devices with their start and end apart: 6, of which 2 were waited for; matrix products, arithmetic and copies ran while one was open for 4% of the time, Pallas kernels for 0%

commit v1 on v0

--- a/solution.py
+++ b/solution.py
@@ -96,7 +96,9 @@
         stacked.astype(jnp.bfloat16), "dom", scatter_dimension=0, tiled=True
     ).astype(jnp.float32)
     mine = summed[:blk]
-    grad_weight = lax.psum(summed[blk:].astype(jnp.bfloat16), "cluster").astype(jnp.float32)
+    grad_weight = jnp.sum(
+        lax.all_gather(summed[blk:].astype(jnp.bfloat16), "cluster"), axis=0
+    ).astype(jnp.float32)
     bgrad = mine + from_upper + from_lower
     full = dagg.astype(jnp.float32)
     current = lax.dynamic_slice_in_dim(full, start_row, blk, 0)

time: 194 us -> 167 us (0.86)
  waiting for transfers between devices: 93.6 us -> 63.4 us
  blocking collectives: 31.9 us -> 37.6 us
    psum x1 -> x0, waiting for transfers between devices: 30.2 us -> none  [per_device(): lax.psum(summed[blk:].astype(jnp.bfloat16), 'cluster').astype(jnp.float32)]
    all_gather x0 -> x1, blocking collectives: none -> 5.76 us  [per_device(): lax.all_gather(summed[blk:].astype(jnp.bfloat16), 'cluster')]
    ppermute x2, waiting for transfers between devices: 0.01 us -> 3.22 us  [passed_along(): return lax.ppermute(x, axis, [(i, (i + by) % count) for i in range(count)])]
    reduce_scatter x1, waiting for transfers between devices: 63.3 us -> 60.2 us  [per_device(): lax.psum_scatter(stacked.astype(jnp.bfloat16), 'dom', scatter_dimension=0...]
  transfers between devices with their start and end apart: 6 -> 5, of which waited for: 2 -> 3; matrix products, arithmetic and copies ran while one was open for 4% -> 3% of each run, Pallas kernels for 0% -> 0%
where the time goes in v1:
time: 167 us
  waiting for transfers between devices  63.4 us (38%)
  blocking collectives  37.6 us (23%)
  matrix products  20.5 us (12%)
  local copies, waits for them, and re-layouts  17.7 us (11%)
  between operations  15.6 us (9%)
  other arithmetic  8.95 us (5%)
  starting transfers between devices  3 us (2%)
    reduce_scatter x1, waiting for transfers between devices, per_device(): lax.psum_scatter(stacked.astype(jnp.bfloat16), 'dom', scatter_dimension=0...  60.2 us
    all_gather x1, blocking collectives, per_device(): lax.all_gather(own_block, 'dom', axis=0, tiled=True)  31.9 us
    dot_general x1, local copies, waits for them, and re-layouts, per_device(): jnp.einsum('wnz,wnx->wzx', tile_blocks, selected_block, preferred_element...  10.3 us
    dot_general x1, matrix products, per_device(): jnp.einsum('xn,xij->nij', row_onehot_mask, contribution, precision=lax.Pr...  6.78 us
    all_gather x1, blocking collectives, per_device(): lax.all_gather(summed[blk:].astype(jnp.bfloat16), 'cluster')  5.76 us
    dot_general x1, matrix products, per_device(): jnp.einsum('wnz,wnx->wzx', tile_blocks, selected_block, preferred_element...  4.62 us
  transfers between devices with their start and end apart: 5, of which 3 were waited for; matrix products, arithmetic and copies ran while one was open for 3% of the time, Pallas kernels for 0%

profile of v1, /device:TPU:0, one launch (start us, length us, event | category | flops | bytes accessed | tf_op | source)
XLA Modules:
  0.0 166.8 jit_solution(3950901149765136928)
XLA Ops:
  7.2 0.0 copy-start
  7.2 0.0 reduce-scatter.2.cloned.1.call-start
  8.0 0.8 constant_dynamic-slice_fusion
  8.7 0.5 collective-permute-start
  9.2 1.9 %collective-permute-start.1 = (bf16[1,32,512]{2,1,0:T(8,128)(2,1)S(1)}, bf16[1,32,512]{2,1,0:T(8,128)(2,1)S(1)}, u32[]{:S(2)}, u32[]{:S(2)}) collective-permute-start(bf16[1,32,512]{2,1,0:T(8,128)(2,1)S(1)} %constant_dynamic-slice_fusion), channel_id=1, source_target_pairs={{1,0},{2,1},{3,2},{0,3},{5,4},{6,5},{7,6},{4,7},{9,8},{10,9},{11,1... | collective-permute-start | bytes 98312 | tf_op jit(solution)/shard_map/ppermute | solution.py:16
  11.1 31.9 %all-gather = bf16[1,256,512]{2,1,0:T(8,128)(2,1)S(1)} all-gather(bf16[1,32,512]{2,1,0:T(8,128)(2,1)S(1)} %constant_dynamic-slice_fusion), channel_id=2, replica_groups=mesh['dom'=8,'cluster'=4] {'dom'}, dimensions={1}, use_global_device_ids=true | all-gather | bytes 294912 | tf_op jit(solution)/shard_map/all_gather | solution.py:45
  43.0 0.7 fusion.30
  43.7 0.7 compare_and_fusion.1
  44.3 0.7 fusion.31
  45.0 0.7 compare_and_fusion
  45.7 0.7 compare_bitcast_fusion
  46.3 0.7 convert_subtract_fusion
  47.7 1.1 broadcast_select_fusion
  48.7 0.0 collective-permute-done
  48.7 0.0 collective-permute-done.1
  48.8 0.6 gather_fusion
  49.4 4.6 %fusion.13 = f32[32,512,128]{2,1,0:T(8,128)} fusion(bf16[32,32,512]{2,1,0:T(8,128)(2,1)S(1)} %gather_fusion, pred[32]{0:T(512)(128)(4,1)S(1)} %compare_and_fusion.1, bf16[1,32,32,128]{3,2,1,0:T(8,128)(2,1)S(1)} %copy-done.1), kind=kOutput, calls=%fused_computation.22 | convolution fusion | flops 134742016 | bytes 9699360 | tf_op jit(solution)/shard_map/wnz,wnx->wzx/dot_general | solution.py:55
  54.1 10.3 %copy.20 = f32[32,512,128]{1,0,2:T(8,128)} copy(f32[32,512,128]{2,1,0:T(8,128)} %fusion.13) | data formatting | bytes 16777216 | tf_op jit(solution)/shard_map/wnz,wnx->wzx/dot_general | solution.py:55
  64.4 6.8 %fusion = f32[6,128,512]{2,0,1:T(8,128)S(1)} fusion(f32[32,512,128]{1,0,2:T(8,128)} %copy.20, f32[32]{0:T(128)S(1)} %compare_convert_fusion, s32[32]{0:T(128)S(1)} %bitcast.74), kind=kOutput, calls=%fused_computation.2 | convolution fusion | flops 153092480 | bytes 9961728 | tf_op jit(solution)/shard_map/xn,xij->nij/dot_general | solution.py:62
  71.1 0.0 copy-start.2
  71.2 0.9 copy.16
  72.1 0.2 copy-done.2
  72.3 0.3 fusion.11
  72.6 1.2 copy.17
  73.8 0.0 copy-done
  73.8 2.0 %fusion.10 = (bf16[768,512]{1,0:T(8,128)(2,1)S(1)}, bf16[1,768,512]{2,1,0:T(8,128)(2,1)}) fusion(bf16[1,768,512]{2,1,0:T(8,128)(2,1)S(1)} %copy-done.7, bf16[768,512]{1,0:T(8,128)(2,1)S(1)} %fusion.11, bf16[512,512]{1,0:T(8,128)(2,1)S(1)} %copy-done), kind=kOutput, calls=%fused_computation.14 | convolution fusion | flops 407371776 | bytes 3670016 | tf_op jit(solution)/shard_map/dot_general | solution.py:68
  75.7 0.6 fusion.35
  76.4 0.5 copy-done.3
  76.9 1.4 convolution_convert_fusion.1
  78.2 2.8 %gather_fusion.1 = bf16[32,128,512]{2,1,0:T(8,128)(2,1)} fusion(bf16[6,128,512]{2,1,0:T(8,128)(2,1)S(1)} %bitcast.67, s32[1024]{0:T(1024)S(1)} %pad_clamp_fusion), kind=kCustom, calls=%fused_computation.1 | custom fusion | bytes 8388736 | tf_op jit(solution)/shard_map/jit(_take)/gather | solution.py:75
  81.0 3.1 %fusion.3 = f32[32,512,32]{1,2,0:T(8,128)S(1)} fusion(bf16[32,128,512]{2,1,0:T(8,128)(2,1)} %gather_fusion.1, pred[32]{0:T(512)(128)(4,1)S(1)} %compare_and_fusion, bf16[1,32,32,128]{3,2,1,0:T(8,128)(2,1)S(1)} %copy-done.1), kind=kOutput, calls=%fused_computation.5 | convolution fusion | flops 136314880 | bytes 6553632 | tf_op jit(solution)/shard_map/dck,dkn->dcn/dot_general | solution.py:77
  84.1 0.0 copy-start.4
  84.1 2.0 %fusion.7 = f32[10,32,512]{2,0,1:T(8,128)S(1)} fusion(f32[32,512,32]{1,2,0:T(8,128)S(1)} %fusion.3, f32[32]{0:T(128)S(1)} %compare_convert_fusion, s32[32]{0:T(128)S(1)} %bitcast.75), kind=kOutput, calls=%fused_computation.9 | convolution fusion | flops 63439168 | bytes 2752768 | tf_op jit(solution)/shard_map/ts,tbf->sbf/dot_general | solution.py:83
  86.2 0.1 fusion.18
  86.3 0.1 copy.18
  86.4 0.0 copy-done.4
  86.4 1.0 pad_maximum_fusion
  87.3 0.0 reduce-scatter.2.cloned.1.call-update
  87.4 0.4 copy.27
  87.7 0.1 collective-permute-start.2
  87.8 0.5 collective-permute-start.3
  88.3 1.1 collective-permute-done.2
  89.4 2.1 %collective-permute-done.3 = bf16[32,512]{1,0:T(8,128)(2,1)S(1)} collective-permute-done((bf16[32,512]{1,0:T(8,128)(2,1)S(1)}, bf16[32,512]{1,0:T(8,128)(2,1)S(1)}, u32[]{:S(2)}, u32[]{:S(2)}) %collective-permute-start.3) | collective-permute-done | bytes 32800 | tf_op jit(solution)/shard_map/ppermute | solution.py:25
  91.5 60.2 %reduce-scatter.2.cloned.1.call-done = bf16[96,512]{1,0:T(8,128)(2,1)} async-done(((bf16[768,512]{1,0:T(8,128)(2,1)}), bf16[96,512]{1,0:T(8,128)(2,1)}) %reduce-scatter.2.cloned.1.call-update) | async-done | bytes 98320 | tf_op jit(solution)/shard_map/reduce_scatter | solution.py:95
  151.7 0.8 add_dynamic-update-slice_fusion
  152.5 1.0 convert_bitcast_fusion
  153.5 5.8 %all-gather.1 = bf16[256,512]{1,0:T(8,128)(2,1)S(1)} all-gather(bf16[64,512]{1,0:T(8,128)(2,1)S(1)} %slice-done), channel_id=3, replica_groups=mesh['dom'=8,'cluster'=4] {'cluster'}, dimensions={0}, use_global_device_ids=true | all-gather | bytes 327680 | tf_op jit(solution)/shard_map/all_gather | solution.py:100
  159.3 0.7 convert_element_type.92
  (17 shorter events, 0.1 us)
Async XLA Ops:
  7.2 66.6 %copy-start = (bf16[512,512]{1,0:T(8,128)(2,1)S(1)}, bf16[512,512]{1,0:T(8,128)(2,1)}, u32[]{:S(2)}) copy-start(bf16[512,512]{1,0:T(8,128)(2,1)} %param.18) | copy-start | bytes 1572868
  7.2 42.2 %copy-start.1 = (bf16[1,32,32,128]{3,2,1,0:T(8,128)(2,1)S(1)}, bf16[1,32,32,128]{3,2,1,0:T(8,128)(2,1)}, u32[]{:S(2)}) copy-start(bf16[1,32,32,128]{3,2,1,0:T(8,128)(2,1)} %param.14) | copy-start | bytes 786436
  7.2 144.5 %reduce-scatter.2.cloned.1.call-start = ((), (), s32[]{:S(2)}) async-start(), calls=%async_computation.1 | async-start | bytes 884736 | tf_op jit(solution)/shard_map/reduce_scatter | solution.py:95
  8.7 40.0 %collective-permute-start = (bf16[1,32,512]{2,1,0:T(8,128)(2,1)S(1)}, bf16[1,32,512]{2,1,0:T(8,128)(2,1)S(1)}, u32[]{:S(2)}, u32[]{:S(2)}) collective-permute-start(bf16[1,32,512]{2,1,0:T(8,128)(2,1)S(1)} %constant_dynamic-slice_fusion), channel_id=1, source_target_pairs={{0,1},{1,2},{2,3},{3,0},{4,5},{5,6},{6,7},{7,4},{8,9},{9,10},{10,1... | collective-permute-start | bytes 98312 | tf_op jit(solution)/shard_map/ppermute | solution.py:14
  9.2 39.5 %collective-permute-start.1 = (bf16[1,32,512]{2,1,0:T(8,128)(2,1)S(1)}, bf16[1,32,512]{2,1,0:T(8,128)(2,1)S(1)}, u32[]{:S(2)}, u32[]{:S(2)}) collective-permute-start(bf16[1,32,512]{2,1,0:T(8,128)(2,1)S(1)} %constant_dynamic-slice_fusion), channel_id=1, source_target_pairs={{1,0},{2,1},{3,2},{0,3},{5,4},{6,5},{7,6},{4,7},{9,8},{10,9},{11,1... | collective-permute-start | bytes 98312 | tf_op jit(solution)/shard_map/ppermute | solution.py:16
  54.1 10.3 %copy-start.5 = (s32[1,32]{1,0:T(1,128)S(1)}, s32[1,32]{1,0:T(1,128)}, u32[]{:S(2)}) copy-start(s32[1,32]{1,0:T(1,128)} %param.15) | copy-start | bytes 388
  71.1 1.1 copy-start.2
  72.3 1.5 copy-start.7
  75.7 1.1 copy-start.3
  81.0 3.1 %copy-start.6 = (s32[1,32]{1,0:T(1,128)S(1)}, s32[1,32]{1,0:T(1,128)}, u32[]{:S(2)}) copy-start(s32[1,32]{1,0:T(1,128)} %param.16) | copy-start | bytes 388
  84.1 2.2 %copy-start.4 = (bf16[8,64,512]{2,1,0:T(8,128)(2,1)S(1)}, bf16[8,64,512]{2,1,0:T(8,128)(2,1)}, u32[]{:S(2)}) copy-start(bf16[8,64,512]{2,1,0:T(8,128)(2,1)} %convolution_convert_fusion.1) | copy-start | bytes 1572868
  87.7 1.7 collective-permute-start.2
  87.8 3.7 %collective-permute-start.3 = (bf16[32,512]{1,0:T(8,128)(2,1)S(1)}, bf16[32,512]{1,0:T(8,128)(2,1)S(1)}, u32[]{:S(2)}, u32[]{:S(2)}) collective-permute-start(bf16[32,512]{1,0:T(8,128)(2,1)S(1)} %get-tuple-element.6), channel_id=1, source_target_pairs={{0,1},{1,2},{2,3},{3,0},{4,5},{5,6},{6,7},{7,4},{8,9},{9,10},{10,1... | collective-permute-start | bytes 98312 | tf_op jit(solution)/shard_map/ppermute | solution.py:25
  151.7 1.8 %slice-start = ((bf16[96,512]{1,0:T(8,128)(2,1)}), bf16[64,512]{1,0:T(8,128)(2,1)S(1)}, s32[]{:S(2)}) async-start(bf16[96,512]{1,0:T(8,128)(2,1)} %reduce-scatter.2.cloned.1.call-done), calls=%async_computation.2 | async-start | bytes 131072 | tf_op jit(solution)/shard_map/slice | solution.py:100
Sparse Core Ops, SparseCore 0:
  87.5 64.1 reduce-scatter.1
